TPU v7x, 512 devices: a whole 4x8x8 slice. The times are simulated.
512 devices in a mesh: row: 8 (over y), col: 64 (over z, x, core).
Axes of the slice: x: 4, y: 8, z: 8, core: 2. Of those that a mesh axis runs over, the one named last changes fastest.
Arguments:
- eigen_slab: float32 [8192, 65536], P('row', 'col'), may hold values from -6 to 6
- secular_poles: float32 [131072], P('col'), may hold values from 0 to 4, as said below
- coupling: float32 [131072], P('col'), may hold values from -7 to 7
- window_roots: float32 [128], replicated, may hold values from 0 to 4, as said below
- deflated: int32 [131072], P('col'), may hold values 0 or 1
- column_map: int32 [131072], P('col'), may hold values from 0 to 131071, as said below
Outputs:
- vectors: float32 [8192, 128], P(('row', 'col'))
Inputs may be any that keep to these rules, and one draw needn't show every extreme that they name: `column_map`: A permutation of the 131072 columns. Grid column c holds columns c * 1024 to (c + 1) * 1024 - 1 and 65536 + c * 1024 to 65536 + (c + 1) * 1024 - 1 of the slab, and positions c * 2048 to (c + 1) * 2048 - 1. Of one grid column's positions, exactly 64 map to the columns of one grid column, 32 to each of 62 others, none to the remaining one. `secular_poles`: each pole lies between (k + 0.2) * 4 / 256 and (k + 0.8) * 4 / 256 for a whole number k. `window_roots`: each root lies within 0.15 * 4 / 256 of k * 4 / 256 for a whole number k of 1 to 255.
All inputs are finite; a program needn't handle non-finite values. No bound on the sum of `deflated` on one device may be relied on, other than what follows from the above.
Results may differ from a plain program's by a relative error of at most 0.0003.
Values sent between devices are 32-bit elements; how exact they have to be, the bound alone decides.
A program may use at most 64 MiB of HBM per device.

v0:
```python
import jax
import jax.numpy as jnp
from jax import lax
from jax.sharding import PartitionSpec as P


def slot_plan(column_map, groups, cols_dev, capacity):
    block_len = column_map.shape[0]
    half_order = cols_dev * groups
    within = column_map % half_order
    target = within // cols_dev
    target_local = within % cols_dev + jnp.where(column_map >= half_order, cols_dev, 0)
    onehot = (target[:, None] == jnp.arange(groups, dtype=jnp.int32)[None, :]).astype(jnp.int32)
    slot_rank = jnp.sum(jnp.cumsum(onehot, axis=0) * onehot, axis=1) - 1
    slot_index = target * capacity + slot_rank
    sentinel = jnp.full((groups * capacity,), block_len, jnp.int32)
    slot_source = sentinel.at[slot_index].set(jnp.arange(block_len, dtype=jnp.int32))
    slot_target = sentinel.at[slot_index].set(target_local)
    return (slot_source, slot_target)


def route_rows(scaled, column_map, groups, cols_dev, capacity):
    slot_source, slot_target = slot_plan(column_map, groups, cols_dev, capacity)
    outgoing = jnp.take(scaled, slot_source, axis=0, mode="fill", fill_value=0.0)
    outgoing = outgoing.reshape(groups, capacity, scaled.shape[1])
    arrived, arrived_index = (
        lax.all_to_all(outgoing, "col", split_axis=0, concat_axis=0, tiled=True),
        lax.all_to_all(
            slot_target.reshape(groups, capacity), "col", split_axis=0, concat_axis=0, tiled=True
        ),
    )
    flat_rows = arrived.reshape(groups * capacity, scaled.shape[1])
    return jnp.zeros_like(scaled).at[arrived_index.reshape(-1)].set(flat_rows, mode="drop")


def body(eigen_slab, secular_poles, coupling, window_roots, deflated, column_map):
    groups = lax.axis_size("col")
    row_groups = lax.axis_size("row")
    block_len = secular_poles.shape[0]
    cols_dev = eigen_slab.shape[1]
    capacity = 2 * (block_len // groups)
    distance = secular_poles[:, None] - window_roots[None, :]
    entries = jnp.where(
        deflated[:, None] == 0, coupling[:, None] / distance, jnp.zeros_like(distance)
    )
    sum_squares = lax.psum(jnp.sum(entries * entries, axis=0), "col")
    inverse = lax.rsqrt(sum_squares)
    scaled = entries * inverse[None, :]
    placed = route_rows(scaled, column_map, groups, cols_dev, capacity)
    half_start = jnp.where(lax.axis_index("row") < row_groups // 2, 0, cols_dev)
    half_window = lax.dynamic_slice_in_dim(placed, half_start, cols_dev, 0)
    return lax.psum_scatter(
        jnp.dot(
            eigen_slab,
            half_window,
            precision=lax.Precision.HIGHEST,
            preferred_element_type=jnp.float32,
        ),
        "col",
        scatter_dimension=0,
        tiled=True,
    )


def solution(mesh):
    return jax.shard_map(
        body,
        mesh=mesh,
        in_specs=(P("row", "col"), P("col"), P("col"), P(), P("col"), P("col")),
        out_specs=P(("row", "col"), None),
        check_vma=False,
    )
```

profile of v0, /device:TPU:8, one launch (start us, length us, event | category | flops | bytes accessed | tf_op | source)
XLA Modules:
  0.0 474.1 jit_solution(13782609337282554614)
XLA Ops:
  6.5 0.7 fusion.9
  7.3 18.1 %reduce-window.6 = s32[64,16,128]{2,1,0:T(8,128)S(1)} reduce-window(s32[64,16,128]{2,1,0:T(8,128)S(1)} %fusion.6, s32[]{:T(128)} %constant.68.clone.1), window={size=1x1x128 pad=0_0x0_0x127_0}, to_apply=%region_0.1 | reduce-window | flops 16646144 | bytes 1048580 | tf_op jit(solution)/shard_map/reduce-window
  25.5 0.2 slice.10
  25.7 0.4 copy.14
  26.3 0.2 broadcast_add_fusion
  26.7 8.1 %scatter_custom_fusion = s32[4096]{0:T(1024)S(1)} fusion(s32[2048]{0:T(1024)S(1)} %compare_select_fusion.2, s32[2048]{0:T(1024)S(1)} %get-tuple-element.5, s32[]{:T(128)} %constant.67.clone.1), kind=kCustom, calls=%fused_computation.37 | custom fusion | bytes 16388 | tf_op jit(solution)/shard_map/scatter | solution.py:18
  34.8 0.7 all_to_all.9
  35.5 13.8 %all-to-all-start = ((s32[64,1,64]{2,1,0:T(1,128)}), s32[64,1,64]{2,1,0:T(1,128)S(1)}, u32[]{:S(2)}, u32[]{:S(2)}) async-start(s32[64,1,64]{2,1,0:T(1,128)} %all_to_all.9), calls=%async_computation | async-start | bytes 65536 | tf_op jit(solution)/shard_map/all_to_all | solution.py:28
  49.3 8.1 %scatter_custom_fusion.1 = s32[4096]{0:T(1024)S(1)} fusion(s32[2048]{0:T(1024)S(1)} %compare_select_fusion.2, s32[2048]{0:T(1024)S(1)} %iota.11, s32[]{:T(128)} %constant.67.clone.1), kind=kCustom, calls=%fused_computation.35 | custom fusion | bytes 16388 | tf_op jit(solution)/shard_map/scatter | solution.py:17
  57.5 1.0 multiply_reduce_fusion
  58.4 129.0 %psum.7 = f32[128]{0:T(128)S(1)} all-reduce(f32[128]{0:T(128)S(1)} %multiply_reduce_fusion), channel_id=1, replica_groups=mesh['row'=8,'col'=64] {'col'}, use_global_device_ids=true, to_apply=%region_6.7 | all-reduce | flops 128 | bytes 1024 | tf_op jit(solution)/shard_map/psum | solution.py:46
  187.4 0.9 fusion
  188.4 10.8 %gather_fusion = f32[4096,128]{1,0:T(8,128)S(1)} fusion(f32[2048,128]{1,0:T(8,128)S(1)} %fusion, s32[4096]{0:T(1024)S(1)} %fusion.7), kind=kCustom, calls=%fused_computation | custom fusion | bytes 4210688 | tf_op jit(solution)/shard_map/jit(_take)/gather | solution.py:24
  199.2 1.7 broadcast_select_fusion
  200.9 5.3 %all-to-all-start.1 = ((f32[64,64,128]{2,1,0:T(8,128)}), f32[64,64,128]{2,1,0:T(8,128)S(1)}, u32[]{:S(2)}, u32[]{:S(2)}) async-start(f32[64,64,128]{2,1,0:T(8,128)} %broadcast_select_fusion), calls=%async_computation.1 | async-start | bytes 4194304 | tf_op jit(solution)/shard_map/all_to_all | solution.py:27
  206.3 0.5 broadcast.104
  206.8 0.7 reduce.3
  207.7 49.9 %all-to-all-done.1 = f32[64,64,128]{2,1,0:T(8,128)S(1)} async-done(((f32[64,64,128]{2,1,0:T(8,128)}), f32[64,64,128]{2,1,0:T(8,128)S(1)}, u32[]{:S(2)}, u32[]{:S(2)}) %all-to-all-start.1) | async-done | bytes 2097184 | tf_op jit(solution)/shard_map/all_to_all | solution.py:27
  257.6 11.0 %scatter_custom_fusion.2 = f32[2048,128]{1,0:T(8,128)S(1)} fusion(s32[4096]{0:T(1024)S(1)} %bitcast.32, f32[4096,128]{1,0:T(8,128)S(1)} %bitcast.27, f32[]{:T(128)} %constant.66.clone.1), kind=kCustom, calls=%fused_computation.15 | custom fusion | bytes 1048580 | tf_op jit(solution)/shard_map/scatter | solution.py:33
  268.7 7.5 %convolution_bitcast_fusion = f32[1024,128]{0,1:T(8,128)} fusion(f32[1024,1024]{1,0:T(8,128)} %param.6, f32[2048,128]{1,0:T(8,128)S(1)} %scatter_custom_fusion.2, s32[]{:T(128)S(6)} %select_n.62), kind=kOutput, calls=%fused_computation.4 | convolution fusion | flops 1610612736 | bytes 5242884 | tf_op jit(solution)/shard_map/dot_general | solution.py:53
  276.2 1.3 dynamic-slice
  278.1 187.6 %all-reduce.3.cloned.1.call-done = f32[1024,128]{0,1:T(8,128)} async-done(((f32[1024,128]{0,1:T(8,128)}), f32[1024,128]{0,1:T(8,128)}) %all-reduce.3.cloned.1.call-update) | async-done | bytes 524304
  465.7 0.9 constant_dynamic-slice_fusion
  466.6 0.7 copy.13
  (23 shorter events, 0.7 us)
Async XLA Ops:
  7.3 50.1 %copy-start.2 = (s32[2048]{0:T(1024)S(1)}, s32[2048]{0:T(1024)}, u32[]{:S(2)}) copy-start(s32[2048]{0:T(1024)} %param.10) | copy-start | bytes 24580
  7.3 50.1 %copy-start = (f32[2048]{0:T(1024)S(1)}, f32[2048]{0:T(1024)}, u32[]{:S(2)}) copy-start(f32[2048]{0:T(1024)} %param.7) | copy-start | bytes 24580
  7.3 50.1 %copy-start.1 = (f32[2048]{0:T(1024)S(1)}, f32[2048]{0:T(1024)}, u32[]{:S(2)}) copy-start(f32[2048]{0:T(1024)} %param.8) | copy-start | bytes 24580
  7.3 50.1 %copy-start.3 = (f32[128]{0:T(128)S(1)}, f32[128]{0:T(128)}, u32[]{:S(2)}) copy-start(f32[128]{0:T(128)} %param.9) | copy-start | bytes 1540
  35.5 165.4 %all-to-all-start = ((s32[64,1,64]{2,1,0:T(1,128)}), s32[64,1,64]{2,1,0:T(1,128)S(1)}, u32[]{:S(2)}, u32[]{:S(2)}) async-start(s32[64,1,64]{2,1,0:T(1,128)} %all_to_all.9), calls=%async_computation | async-start | bytes 65536 | tf_op jit(solution)/shard_map/all_to_all | solution.py:28
  200.9 56.7 %all-to-all-start.1 = ((f32[64,64,128]{2,1,0:T(8,128)}), f32[64,64,128]{2,1,0:T(8,128)S(1)}, u32[]{:S(2)}, u32[]{:S(2)}) async-start(f32[64,64,128]{2,1,0:T(8,128)} %broadcast_select_fusion), calls=%async_computation.1 | async-start | bytes 4194304 | tf_op jit(solution)/shard_map/all_to_all | solution.py:27
  206.3 259.4 %all-reduce.3.cloned.1.call-start = ((), (), s32[]{:S(2)}) async-start(), calls=%async_computation.2 | async-start | bytes 1048576
Sparse Core Ops, SparseCore 0:
  276.3 189.3 all-reduce.2
where the time goes:
time: 475 us; the launch traced here: 474 us
  waiting for transfers between devices  238 us (50%)
  blocking collectives  129 us (27%)
  local copies, waits for them, and re-layouts  42.8 us (9%)
  other arithmetic  23.9 us (5%)
  starting transfers between devices  19.2 us (4%)
  between operations  14.3 us (3%)
  matrix products  7.48 us (2%)
    unnamed x2, waiting for transfers between devices  188 us
    psum x1, blocking collectives, body(): sum_squares = lax.psum(jnp.sum(entries * entries, axis=0), 'col')  129 us
    all_to_all x1, waiting for transfers between devices, route_rows(): lax.all_to_all(outgoing, 'col', split_axis=0, concat_axis=0, tiled=True)  49.9 us
    another operation x3, other arithmetic  18.5 us
    all_to_all x1, starting transfers between devices, route_rows(): lax.all_to_all(slot_target.reshape(groups, capacity), 'col', split_axis=0...  13.8 us
    scatter x1, local copies, waits for them, and re-layouts, route_rows(): jnp.zeros_like(scaled).at[arrived_index.reshape(-1)]  11 us
    gather x1, local copies, waits for them, and re-layouts, route_rows(): jnp.take(scaled, slot_source, axis=0, mode='fill', fill_value=0.0)  10.8 us
  transfers between devices with their start and end apart: 3, of which 2 were waited for; matrix products, arithmetic and copies ran while one was open for 5% of the time, Pallas kernels for 0%

commit v1 on v0

--- a/solution.py
+++ b/solution.py
@@ -43,7 +43,7 @@
     entries = jnp.where(
         deflated[:, None] == 0, coupling[:, None] / distance, jnp.zeros_like(distance)
     )
-    sum_squares = lax.psum(jnp.sum(entries * entries, axis=0), "col")
+    sum_squares = jnp.sum(lax.all_gather(jnp.sum(entries * entries, axis=0), "col"), axis=0)
     inverse = lax.rsqrt(sum_squares)
     scaled = entries * inverse[None, :]
     placed = route_rows(scaled, column_map, groups, cols_dev, capacity)

time: 475 us -> 388 us (0.82)
  blocking collectives: 129 us -> 41 us
    psum x1 -> x0, blocking collectives: 129 us -> none  [body(): sum_squares = lax.psum(jnp.sum(entries * entries, axis=0), 'col')]
    all_gather x0 -> x1, blocking collectives: none -> 41 us  [body(): lax.all_gather(jnp.sum(entries * entries, axis=0), 'col')]
  transfers between devices with their start and end apart: 3 -> 3, of which waited for: 2 -> 2; matrix products, arithmetic and copies ran while one was open for 5% -> 7% of each run, Pallas kernels for 0% -> 0%
where the time goes in v1:
time: 388 us
  waiting for transfers between devices  238 us (61%)
  local copies, waits for them, and re-layouts  42.8 us (11%)
  blocking collectives  41 us (11%)
  other arithmetic  23.9 us (6%)
  starting transfers between devices  20.6 us (5%)
  between operations  14.3 us (4%)
  matrix products  7.48 us (2%)
    unnamed x2, waiting for transfers between devices  188 us
    all_to_all x1, waiting for transfers between devices, route_rows(): lax.all_to_all(outgoing, 'col', split_axis=0, concat_axis=0, tiled=True)  49.9 us
    all_gather x1, blocking collectives, body(): lax.all_gather(jnp.sum(entries * entries, axis=0), 'col')  41 us
    another operation x3, other arithmetic  18.5 us
    all_to_all x1, starting transfers between devices, route_rows(): lax.all_to_all(slot_target.reshape(groups, capacity), 'col', split_axis=0...  13.8 us
    scatter x1, local copies, waits for them, and re-layouts, route_rows(): jnp.zeros_like(scaled).at[arrived_index.reshape(-1)]  11 us
    gather x1, local copies, waits for them, and re-layouts, route_rows(): jnp.take(scaled, slot_source, axis=0, mode='fill', fill_value=0.0)  10.8 us
    scatter x1, local copies, waits for them, and re-layouts, slot_plan(): slot_target = sentinel.at[slot_index].set(target_local)  8.06 us
  transfers between devices with their start and end apart: 3, of which 2 were waited for; matrix products, arithmetic and copies ran while one was open for 7% of the time, Pallas kernels for 0%

profile of v1, /device:TPU:8, one launch (start us, length us, event | category | flops | bytes accessed | tf_op | source)
XLA Modules:
  0.0 387.9 jit_solution(18025468665197989754)
XLA Ops:
  6.5 0.7 fusion.9
  7.3 18.1 %reduce-window.6 = s32[64,16,128]{2,1,0:T(8,128)S(1)} reduce-window(s32[64,16,128]{2,1,0:T(8,128)S(1)} %fusion.6, s32[]{:T(128)} %constant.68.clone.1), window={size=1x1x128 pad=0_0x0_0x127_0}, to_apply=%region_0.1 | reduce-window | flops 16646144 | bytes 1048580 | tf_op jit(solution)/shard_map/reduce-window
  25.5 0.2 slice.10
  25.7 0.4 copy.14
  26.3 0.2 broadcast_add_fusion
  26.7 8.1 %scatter_custom_fusion = s32[4096]{0:T(1024)S(1)} fusion(s32[2048]{0:T(1024)S(1)} %compare_select_fusion.2, s32[2048]{0:T(1024)S(1)} %get-tuple-element.5, s32[]{:T(128)} %constant.67.clone.1), kind=kCustom, calls=%fused_computation.37 | custom fusion | bytes 16388 | tf_op jit(solution)/shard_map/scatter | solution.py:18
  34.8 0.7 all_to_all.9
  35.5 13.8 %all-to-all-start = ((s32[64,1,64]{2,1,0:T(1,128)}), s32[64,1,64]{2,1,0:T(1,128)S(1)}, u32[]{:S(2)}, u32[]{:S(2)}) async-start(s32[64,1,64]{2,1,0:T(1,128)} %all_to_all.9), calls=%async_computation | async-start | bytes 65536 | tf_op jit(solution)/shard_map/all_to_all | solution.py:28
  49.3 8.1 %scatter_custom_fusion.1 = s32[4096]{0:T(1024)S(1)} fusion(s32[2048]{0:T(1024)S(1)} %compare_select_fusion.2, s32[2048]{0:T(1024)S(1)} %iota.11, s32[]{:T(128)} %constant.67.clone.1), kind=kCustom, calls=%fused_computation.35 | custom fusion | bytes 16388 | tf_op jit(solution)/shard_map/scatter | solution.py:17
  57.5 1.0 multiply_reduce_fusion
  58.4 41.0 %all-gather.1 = f32[64,1,128]{2,1,0:T(1,128)S(1)} all-gather(f32[1,1,128]{2,1,0:T(1,128)S(1)} %bitcast.34), channel_id=2, replica_groups=mesh['row'=8,'col'=64] {'col'}, dimensions={0}, use_global_device_ids=true | all-gather | bytes 33280 | tf_op jit(solution)/shard_map/all_gather | solution.py:46
  99.5 0.9 fusion
  100.5 10.8 %gather_fusion = f32[4096,128]{1,0:T(8,128)S(1)} fusion(f32[2048,128]{1,0:T(8,128)S(1)} %fusion, s32[4096]{0:T(1024)S(1)} %fusion.7), kind=kCustom, calls=%fused_computation | custom fusion | bytes 4210688 | tf_op jit(solution)/shard_map/jit(_take)/gather | solution.py:24
  111.3 1.7 broadcast_select_fusion
  113.0 6.7 %all-to-all-start.1 = ((f32[64,64,128]{2,1,0:T(8,128)}), f32[64,64,128]{2,1,0:T(8,128)S(1)}, u32[]{:S(2)}, u32[]{:S(2)}) async-start(f32[64,64,128]{2,1,0:T(8,128)} %broadcast_select_fusion), calls=%async_computation.1 | async-start | bytes 4194304 | tf_op jit(solution)/shard_map/all_to_all | solution.py:27
  119.8 0.5 broadcast.103
  120.3 0.7 reduce.4
  121.2 49.9 %all-to-all-done.1 = f32[64,64,128]{2,1,0:T(8,128)S(1)} async-done(((f32[64,64,128]{2,1,0:T(8,128)}), f32[64,64,128]{2,1,0:T(8,128)S(1)}, u32[]{:S(2)}, u32[]{:S(2)}) %all-to-all-start.1) | async-done | bytes 2097184 | tf_op jit(solution)/shard_map/all_to_all | solution.py:27
  171.1 11.0 %scatter_custom_fusion.2 = f32[2048,128]{1,0:T(8,128)S(1)} fusion(s32[4096]{0:T(1024)S(1)} %bitcast.33, f32[4096,128]{1,0:T(8,128)S(1)} %bitcast.28, f32[]{:T(128)} %constant.66.clone.1), kind=kCustom, calls=%fused_computation.15 | custom fusion | bytes 1048580 | tf_op jit(solution)/shard_map/scatter | solution.py:33
  182.2 7.5 %convolution_bitcast_fusion = f32[1024,128]{0,1:T(8,128)} fusion(f32[1024,1024]{1,0:T(8,128)} %param.6, f32[2048,128]{1,0:T(8,128)S(1)} %scatter_custom_fusion.2, s32[]{:T(128)S(6)} %select_n.62), kind=kOutput, calls=%fused_computation.4 | convolution fusion | flops 1610612736 | bytes 5242884 | tf_op jit(solution)/shard_map/dot_general | solution.py:53
  189.7 1.3 dynamic-slice
  191.6 187.9 %all-reduce.3.cloned.1.call-done = f32[1024,128]{0,1:T(8,128)} async-done(((f32[1024,128]{0,1:T(8,128)}), f32[1024,128]{0,1:T(8,128)}) %all-reduce.3.cloned.1.call-update) | async-done | bytes 524304
  379.5 0.9 constant_dynamic-slice_fusion
  380.4 0.7 copy.13
  (24 shorter events, 0.8 us)
Async XLA Ops:
  7.3 50.1 %copy-start.2 = (s32[2048]{0:T(1024)S(1)}, s32[2048]{0:T(1024)}, u32[]{:S(2)}) copy-start(s32[2048]{0:T(1024)} %param.10) | copy-start | bytes 24580
  7.3 50.1 %copy-start = (f32[2048]{0:T(1024)S(1)}, f32[2048]{0:T(1024)}, u32[]{:S(2)}) copy-start(f32[2048]{0:T(1024)} %param.7) | copy-start | bytes 24580
  7.3 50.1 %copy-start.1 = (f32[2048]{0:T(1024)S(1)}, f32[2048]{0:T(1024)}, u32[]{:S(2)}) copy-start(f32[2048]{0:T(1024)} %param.8) | copy-start | bytes 24580
  7.3 50.1 %copy-start.3 = (f32[128]{0:T(128)S(1)}, f32[128]{0:T(128)}, u32[]{:S(2)}) copy-start(f32[128]{0:T(128)} %param.9) | copy-start | bytes 1540
  35.5 77.5 %all-to-all-start = ((s32[64,1,64]{2,1,0:T(1,128)}), s32[64,1,64]{2,1,0:T(1,128)S(1)}, u32[]{:S(2)}, u32[]{:S(2)}) async-start(s32[64,1,64]{2,1,0:T(1,128)} %all_to_all.9), calls=%async_computation | async-start | bytes 65536 | tf_op jit(solution)/shard_map/all_to_all | solution.py:28
  113.0 58.1 %all-to-all-start.1 = ((f32[64,64,128]{2,1,0:T(8,128)}), f32[64,64,128]{2,1,0:T(8,128)S(1)}, u32[]{:S(2)}, u32[]{:S(2)}) async-start(f32[64,64,128]{2,1,0:T(8,128)} %broadcast_select_fusion), calls=%async_computation.1 | async-start | bytes 4194304 | tf_op jit(solution)/shard_map/all_to_all | solution.py:27
  119.8 259.7 %all-reduce.3.cloned.1.call-start = ((), (), s32[]{:S(2)}) async-start(), calls=%async_computation.2 | async-start | bytes 1048576
Sparse Core Ops, SparseCore 0:
  189.8 189.6 all-reduce.2
